TPU v7x, 32 devices: a whole 2x2x4 slice. The times are simulated.
32 devices in a mesh: region: 4 (over z), tok: 8 (over y, x, core).
Axes of the slice: x: 2, y: 2, z: 4, core: 2. Of those that a mesh axis runs over, the one named last changes fastest.
Arguments:
- tokens: bfloat16 [4096, 1024], P(('region', 'tok')), may hold values from -6 to 6
- w_query: bfloat16 [1024, 1024], P('tok'), may hold values from -0.1875 to 0.1875
- w_key: bfloat16 [1024, 1024], P('tok'), may hold values from -0.1875 to 0.1875
- w_value: bfloat16 [1024, 1024], P('tok'), may hold values from -0.1875 to 0.1875
- w_out: bfloat16 [1024, 1024], P(None, 'tok'), may hold values from -0.1875 to 0.1875
- past_keys: bfloat16 [4, 4096, 1024], P(None, ('region', 'tok')), may hold values from -600 to 600
- past_values: bfloat16 [4, 4096, 1024], P(None, ('region', 'tok')), may hold values from -6 to 6
- nb_block: int32 [32, 8], replicated, may hold values from 0 to 31, as said below
- nb_frame: int32 [32, 8], replicated, may hold values from 0 to 3, as said below
- nb_count: int32 [32], replicated, may hold values from 2 to 8
- block_slot: int32 [32], replicated, may hold values from 0 to 31, as said below
Outputs:
- attn_out: bfloat16 [4096, 1024], P(('region', 'tok'))
Inputs may be any that keep to these rules, and one draw needn't show every extreme that they name: block_slot is a permutation of the block ids; device i of region+tok stores slot i (one block per device). `nb_block`: the entries of one query block name distinct blocks. For the query blocks of device (r, c) of region+tok, entry 0 names one and the same block and frame stored in region group r - 1, entry 1 one and the same stored in group r + 1 (periodic), the other entries blocks stored in group r, on tok indices other than those of entries 0 and 1. For each group r and tok index t, exactly one device of group r reads its entry 0 from tok index t of group r - 1, and exactly one reads its entry 1 from tok index t of group r + 1. All entries of query blocks of devices with tok index c that name blocks stored on one device name one and the same block and frame. `nb_frame`: see nb_block.
All inputs are finite; a program needn't handle non-finite values.
Results may differ from a plain program's by a relative error of at most 0.0035.
The roundings to bfloat16 on the way count: a program that leaves them out, or rounds other values in their place, can miss the bound.
Values may be sent and summed in bfloat16 or wider, within the bound.
No kernel may reach another device: no remote copies, remote signals or barrier semaphores. Data moves between devices by JAX's collectives and lax.ppermute only.
A program may use at most 128 MiB of HBM per device.

v0:
```python
import jax
import jax.numpy as jnp
from jax import lax
from jax.sharding import PartitionSpec as P

HEADS = 8
QB = 128


def shifted(block, axis, distance):
    devices = range(lax.axis_size(axis))
    route = [((i - distance) % len(devices), i) for i in devices]
    return lax.ppermute(block, axis, route)


def per_device(
    tokens,
    w_query,
    w_key,
    w_value,
    w_out,
    past_keys,
    past_values,
    nb_block,
    nb_frame,
    nb_count,
    block_slot,
):
    n_region = lax.axis_size("region")
    n_tok = lax.axis_size("tok")
    region_id = lax.axis_index("region")
    tok_id = lax.axis_index("tok")
    n_devices = n_region * n_tok
    my_device = region_id * n_tok + tok_id
    tok_rows, model_width = tokens.shape
    blocks_dev = tok_rows // QB
    n_blocks, max_entries = nb_block.shape
    head_size = model_width // HEADS
    whole_query, whole_key, whole_value = (
        lax.all_gather(w_query, "tok", axis=0, tiled=True),
        lax.all_gather(w_key, "tok", axis=0, tiled=True),
        lax.all_gather(w_value, "tok", axis=0, tiled=True),
    )
    proj_query = jnp.dot(tokens, whole_query, preferred_element_type=jnp.float32)
    proj_key = jnp.dot(tokens, whole_key, preferred_element_type=jnp.float32)
    proj_value = jnp.dot(tokens, whole_value, preferred_element_type=jnp.float32)
    queries = proj_query.astype(jnp.bfloat16)
    keys_new = proj_key.astype(jnp.bfloat16)
    values_new = proj_value.astype(jnp.bfloat16)
    slot_table = jnp.take(block_slot, nb_block, axis=0)
    source_dev = slot_table // blocks_dev
    source_tok = source_dev % n_tok
    flat_table = nb_frame * blocks_dev + slot_table % blocks_dev
    live_table = jnp.arange(max_entries, dtype=jnp.int32)[None, :] < nb_count[:, None]
    dest_tok = jnp.arange(n_blocks, dtype=jnp.int32) // blocks_dev % n_tok
    tok_range = jnp.arange(n_tok, dtype=jnp.int32)
    mine_flat = (live_table & (source_dev == my_device)).reshape(-1)
    dest_flat = jnp.broadcast_to(dest_tok[:, None], (n_blocks, max_entries)).reshape(-1)
    matches = mine_flat[None, :] & (dest_flat[None, :] == tok_range[:, None])
    offer_index = jnp.max(jnp.where(matches, flat_table.reshape(-1)[None, :], 0), axis=1)
    offer_keys = jnp.take(past_keys, offer_index, axis=0)
    offer_values = jnp.take(past_values, offer_index, axis=0)
    lead_tok = source_tok.reshape(n_devices, blocks_dev, max_entries)[:, 0, :2]
    lower_region = (region_id + n_region - 1) % n_region
    upper_region = (region_id + 1) % n_region
    my_start = my_device * blocks_dev
    my_tok_table = lax.dynamic_slice_in_dim(source_tok, my_start, blocks_dev, 0)
    got_keys, got_values = (
        lax.all_to_all(offer_keys, "tok", split_axis=0, concat_axis=0, tiled=True),
        lax.all_to_all(offer_values, "tok", split_axis=0, concat_axis=0, tiled=True),
    )
    upward_index = lax.dynamic_index_in_dim(
        lead_tok[:, 0], upper_region * n_tok + tok_id, 0, keepdims=False
    )
    downward_index = lax.dynamic_index_in_dim(
        lead_tok[:, 1], lower_region * n_tok + tok_id, 0, keepdims=False
    )
    upward_pair = jnp.concatenate(
        [
            lax.dynamic_slice_in_dim(got_keys, upward_index, 1, 0),
            lax.dynamic_slice_in_dim(got_values, upward_index, 1, 0),
        ],
        0,
    )
    downward_pair = jnp.concatenate(
        [
            lax.dynamic_slice_in_dim(got_keys, downward_index, 1, 0),
            lax.dynamic_slice_in_dim(got_values, downward_index, 1, 0),
        ],
        0,
    )
    below_pair = shifted(upward_pair, "region", 1)
    above_pair = shifted(downward_pair, "region", -1)
    own_index = my_tok_table[:, 2:].reshape(-1)
    own_keys = jnp.take(got_keys, own_index, axis=0).reshape(
        blocks_dev, (max_entries - 2) * QB, model_width
    )
    own_values = jnp.take(got_values, own_index, axis=0).reshape(
        blocks_dev, (max_entries - 2) * QB, model_width
    )
    side_keys = jnp.concatenate([below_pair[0], above_pair[0]], 0)[None]
    side_values = jnp.concatenate([below_pair[1], above_pair[1]], 0)[None]
    far_keys = jnp.concatenate([side_keys, own_keys], 1)
    far_values = jnp.concatenate([side_values, own_values], 1)
    key_list = jnp.concatenate([keys_new.reshape(blocks_dev, QB, model_width), far_keys], 1)
    value_list = jnp.concatenate([values_new.reshape(blocks_dev, QB, model_width), far_values], 1)
    list_len = key_list.shape[1]
    query_heads = queries.reshape(blocks_dev, QB, HEADS, head_size)
    key_heads = key_list.reshape(blocks_dev, list_len, HEADS, head_size)
    value_heads = value_list.reshape(blocks_dev, list_len, HEADS, head_size)
    attn_scale = head_size ** (-0.5)
    scores = (
        jnp.einsum("bqhd,bkhd->bhqk", query_heads, key_heads, preferred_element_type=jnp.float32)
        * attn_scale
    )
    my_counts = lax.dynamic_slice_in_dim(nb_count, my_start, blocks_dev, 0)
    entry_live = jnp.arange(max_entries, dtype=jnp.int32)[None, :] < my_counts[:, None]
    live_mask = jnp.concatenate(
        [jnp.ones((blocks_dev, QB), bool), jnp.repeat(entry_live, QB, axis=1)], 1
    )
    scores = jnp.where(live_mask[:, None, None, :], scores, jnp.float32(-1e30))
    row_max = jnp.max(scores, axis=-1, keepdims=True)
    exp_weights = jnp.where(
        live_mask[:, None, None, :], jnp.exp(scores - row_max), jnp.float32(0.0)
    )
    row_total = jnp.sum(exp_weights, axis=-1)
    prob_bf = exp_weights.astype(jnp.bfloat16)
    context = jnp.einsum(
        "bhqk,bkhd->bqhd", prob_bf, value_heads, preferred_element_type=jnp.float32
    )
    context = context / jnp.swapaxes(row_total, 1, 2)[:, :, :, None]
    context_bf = context.reshape(tok_rows, model_width).astype(jnp.bfloat16)
    whole_out = lax.all_gather(w_out, "tok", axis=1, tiled=True)
    mixed_out = jnp.dot(context_bf, whole_out, preferred_element_type=jnp.float32)
    return mixed_out.astype(jnp.bfloat16)


def solution(mesh):
    return jax.shard_map(
        per_device,
        mesh=mesh,
        in_specs=(
            P(("region", "tok"), None),
            P("tok", None),
            P("tok", None),
            P("tok", None),
            P(None, "tok"),
            P(None, ("region", "tok"), None),
            P(None, ("region", "tok"), None),
            P(),
            P(),
            P(),
            P(),
        ),
        out_specs=P(("region", "tok"), None),
        check_vma=False,
    )
```

profile of v0, /device:TPU:0, one launch (start us, length us, event | category | flops | bytes accessed | tf_op | source)
XLA Modules:
  0.0 164.5 jit_solution(5004245826716925079)
XLA Ops:
  9.7 1.9 %gather_fusion = s32[256]{0:T(256)S(1)} fusion(s32[32]{0:T(128)S(1)} %copy-done.1, s32[1024]{0:T(1024)S(1)} %pad_clamp_fusion.2), kind=kCustom, calls=%fused_computation.4 | custom fusion | bytes 3072 | tf_op jit(solution)/shard_map/jit(_take)/gather | solution.py:50
  13.0 3.3 %gather_fusion.2 = bf16[8,128,1024]{2,1,0:T(8,128)(2,1)} fusion(bf16[4,128,1024]{2,1,0:T(8,128)(2,1)} %param.21, s32[1024]{0:T(1024)S(1)} %pad_clamp_fusion.1), kind=kCustom, calls=%fused_computation.2.clone | custom fusion | bytes 4194336 | tf_op jit(solution)/shard_map/jit(_take)/gather | solution.py:62
  16.3 3.4 %broadcast_select_fusion = (bf16[8,128,1024]{2,1,0:T(8,128)(2,1)S(1)}, bf16[8,128,1024]{2,1,0:T(8,128)(2,1)}) fusion(bf16[8,128,1024]{2,1,0:T(8,128)(2,1)} %gather_fusion.2, pred[8]{0:T(512)(128)(4,1)S(1)} %compare_and_fusion.1, bf16[8,128,1024]{2,1,0:T(8,128)(2,1)S(1)} %gather_fusion.1), kind=kLoop, calls=%fused_computation.26 | loop fusion | flops 2097152 | bytes 8388616 | tf_op jit(solution)/shard_map/jit(_take)/select_n | solution.py:62
  19.7 37.2 %all_to_all.10 = bf16[8,128,1024]{2,1,0:T(8,128)(2,1)S(1)} all-to-all(bf16[8,128,1024]{2,1,0:T(8,128)(2,1)S(1)} %get-tuple-element.21), channel_id=1, replica_groups=mesh['region'=4,'tok'=8] {'tok'}, dimensions={0} | all-to-all | bytes 4194304 | tf_op jit(solution)/shard_map/all_to_all | solution.py:70
  56.9 4.4 %all-to-all-start = ((bf16[8,128,1024]{2,1,0:T(8,128)(2,1)}), bf16[8,128,1024]{2,1,0:T(8,128)(2,1)}, u32[]{:S(2)}, u32[]{:S(2)}) async-start(bf16[8,128,1024]{2,1,0:T(8,128)(2,1)} %get-tuple-element.22), calls=%async_computation | async-start | bytes 4194304 | tf_op jit(solution)/shard_map/all_to_all | solution.py:69
  68.4 26.7 %all-to-all-done = bf16[8,128,1024]{2,1,0:T(8,128)(2,1)} async-done(((bf16[8,128,1024]{2,1,0:T(8,128)(2,1)}), bf16[8,128,1024]{2,1,0:T(8,128)(2,1)}, u32[]{:S(2)}, u32[]{:S(2)}) %all-to-all-start) | async-done | bytes 2097184 | tf_op jit(solution)/shard_map/all_to_all | solution.py:69
  95.0 1.1 constant_dynamic-slice_fusion.5
  96.1 1.8 %pad_maximum_fusion = bf16[2,128,1024]{2,1,0:T(8,128)(2,1)} fusion(bf16[1,128,1024]{2,1,0:T(8,128)(2,1)} %get-tuple-element.11, bf16[1,128,1024]{2,1,0:T(8,128)(2,1)S(1)} %get-tuple-element.9), kind=kLoop, calls=%fused_computation.39 | loop fusion | flops 262144 | bytes 1048576 | tf_op jit(solution)/shard_map/concatenate | solution.py:78
  97.9 1.5 collective-permute-start
  100.3 2.3 %collective-permute-start.1 = (bf16[2,128,1024]{2,1,0:T(8,128)(2,1)}, bf16[2,128,1024]{2,1,0:T(8,128)(2,1)}, u32[]{:S(2)}, u32[]{:S(2)}) collective-permute-start(bf16[2,128,1024]{2,1,0:T(8,128)(2,1)} %pad_maximum_fusion.1), channel_id=1, source_target_pairs={{8,0},{16,8},{24,16},{0,24},{9,1},{17,9},{25,17},{1,25},{10,2},{18... | collective-permute-start | bytes 1572872 | tf_op jit(solution)/shard_map/ppermute | solution.py:13
  102.6 3.5 %gather_fusion.4 = bf16[6,128,1024]{2,1,0:T(8,128)(2,1)} fusion(bf16[8,128,1024]{2,1,0:T(8,128)(2,1)} %all-to-all-done, s32[1024]{0:T(1024)S(1)} %pad_clamp_fusion), kind=kCustom, calls=%fused_computation.3.clone | custom fusion | bytes 3145752 | tf_op jit(solution)/shard_map/jit(_take)/gather | solution.py:95
  106.1 1.9 %gather_fusion.3 = bf16[6,128,1024]{2,1,0:T(8,128)(2,1)} fusion(bf16[8,128,1024]{2,1,0:T(8,128)(2,1)S(1)} %all_to_all.10, s32[1024]{0:T(1024)S(1)} %pad_clamp_fusion), kind=kCustom, calls=%fused_computation.1.clone | custom fusion | bytes 3145752 | tf_op jit(solution)/shard_map/jit(_take)/gather | solution.py:98
  107.9 2.2 %broadcast_select_fusion.3 = (bf16[6,128,1024]{2,1,0:T(8,128)(2,1)S(1)}, bf16[6,128,1024]{2,1,0:T(8,128)(2,1)S(1)}) fusion(bf16[6,128,1024]{2,1,0:T(8,128)(2,1)} %gather_fusion.3, pred[6]{0:T(512)(128)(4,1)S(1)} %get-tuple-element.6, bf16[6,128,1024]{2,1,0:T(8,128)(2,1)} %gather_fusion.4), kind=kLoop, calls=%fused_computation.29 | loop fusion | flops 1572864 | bytes 6291462 | tf_op jit(solution)/shard_map/jit(_take)/select_n | solution.py:98
  110.6 1.4 copy.62
  112.5 1.9 %copy.56 = bf16[1,768,8,128]{1,3,2,0:T(8,128)(2,1)} copy(bf16[1,768,8,128]{3,2,1,0:T(8,128)(2,1)S(1)} %bitcast.77) | data formatting | bytes 3145728 | tf_op jit(solution)/shard_map/concatenate | solution.py:106
  116.2 5.8 %collective-permute-done.1 = bf16[2,128,1024]{2,1,0:T(8,128)(2,1)} collective-permute-done((bf16[2,128,1024]{2,1,0:T(8,128)(2,1)}, bf16[2,128,1024]{2,1,0:T(8,128)(2,1)}, u32[]{:S(2)}, u32[]{:S(2)}) %collective-permute-start.1) | collective-permute-done | bytes 524320 | tf_op jit(solution)/shard_map/ppermute | solution.py:13
  122.0 1.1 fusion.36
  125.2 2.0 %fusion.21 = bf16[16,8,8,128]{3,1,2,0:T(8,128)(2,1)S(1)} fusion(bf16[128,1024]{1,0:T(8,128)(2,1)S(1)} %copy-done.2, bf16[1024,1024]{1,0:T(8,128)(2,1)} %all-gather.9.cloned.1.call-done), kind=kOutput, calls=%fused_computation.36 | convolution fusion | flops 268566528 | bytes 2621440 | tf_op jit(solution)/shard_map/dot_general | solution.py:45
  128.0 2.0 %convolution_convert_fusion.3 = bf16[128,1024]{1,0:T(8,128)(2,1)S(1)} fusion(bf16[128,1024]{1,0:T(8,128)(2,1)S(1)} %copy-done.2, bf16[1024,1024]{1,0:T(8,128)(2,1)} %all-gather.5.cloned.1.call-done), kind=kOutput, calls=%fused_computation.34 | convolution fusion | flops 268566528 | bytes 2621440 | tf_op jit(solution)/shard_map/dot_general | solution.py:46
  130.9 2.0 %fusion.20 = bf16[16,8,8,128]{3,2,1,0:T(8,128)(2,1)S(1)} fusion(bf16[128,1024]{1,0:T(8,128)(2,1)S(1)} %copy-done.2, bf16[1024,1024]{1,0:T(8,128)(2,1)} %all-gather.7.cloned.1.call-done), kind=kOutput, calls=%fused_computation.35 | convolution fusion | flops 268566528 | bytes 2621440 | tf_op jit(solution)/shard_map/dot_general | solution.py:44
  133.0 5.0 %fusion.38 = (f32[8,128]{1,0:T(8,128)S(1)}, bf16[8,128,1152]{2,1,0:T(8,128)(2,1)}) fusion(pred[1152]{0:T(1024)(128)(4,1)S(1)} %pad_reduce_fusion, bf16[1,768,8,128]{3,1,2,0:T(8,128)(2,1)} %copy.62, bf16[1,128,8,128]{3,1,2,0:T(8,128)(2,1)} %copy.61, bf16[1,128,8,128]{3,1,2,0:T(8,128)(2,1)S(1)} %copy.60, bf16[1,128,8,128]{3,1,2,0:T(8,128)(2,1)} %copy.59, ...), kind=kOutput, calls=%fused_computation.78 | convolution fusion | flops 318506112 | bytes 4985984 | tf_op jit(solution)/shard_map/sub | solution.py:124
  137.9 2.8 %fusion.25 = bf16[1,128,8,128]{1,3,2,0:T(8,128)(2,1)S(1)} fusion(bf16[8,128,1152]{2,1,0:T(8,128)(2,1)} %get-tuple-element.24, bf16[1,768,8,128]{1,3,2,0:T(8,128)(2,1)S(1)} %copy-done.3, bf16[1,128,8,128]{1,3,2,0:T(8,128)(2,1)} %bitcast.85, bf16[1,128,8,128]{1,3,2,0:T(8,128)(2,1)S(1)} %bitcast.84, bf16[1,128,8,128]{1,3,2,0:T(8,128)(2,1)} %bitcast.86, ...), kind=kOutput, calls=%fused_computation.38 | convolution fusion | flops 311689216 | bytes 4984832 | tf_op jit(solution)/shard_map/bhqk,bkhd->bqhd/dot_general | solution.py:128
  140.7 14.5 %all-gather.11.cloned.1.call-done = bf16[1024,1024]{1,0:T(8,128)(2,1)} async-done(((bf16[1024,128]{1,0:T(8,128)(2,1)}), bf16[1024,1024]{1,0:T(8,128)(2,1)}) %all-gather.11.cloned.1.call-update) | async-done | bytes 2097168 | tf_op jit(solution)/shard_map/all_gather | solution.py:133
  155.2 2.8 %convolution_convert_fusion = bf16[128,1024]{1,0:T(8,128)(2,1)} fusion(bf16[128,1024]{0,1:T(8,128)(2,1)S(1)} %bitcast.83, bf16[1024,1024]{1,0:T(8,128)(2,1)} %all-gather.11.cloned.1.call-done), kind=kOutput, calls=%fused_computation.31 | convolution fusion | flops 268566528 | bytes 2621440 | tf_op jit(solution)/shard_map/dot_general | solution.py:134
  (67 shorter events, 15.2 us)
Async XLA Ops:
  6.5 5.8 %copy-start = (bf16[4,128,1024]{2,1,0:T(8,128)(2,1)S(1)}, bf16[4,128,1024]{2,1,0:T(8,128)(2,1)}, u32[]{:S(2)}) copy-start(bf16[4,128,1024]{2,1,0:T(8,128)(2,1)} %param.20) | copy-start | bytes 3145732
  6.5 3.1 %copy-start.1 = (s32[32]{0:T(128)S(1)}, s32[32]{0:T(128)}, u32[]{:S(2)}) copy-start(s32[32]{0:T(128)} %param.25) | copy-start | bytes 388
  6.5 118.6 %all-gather.9.cloned.1.call-start = ((), (), s32[]{:S(2)}) async-start(), calls=%async_computation.4 | async-start | bytes 2359296 | tf_op jit(solution)/shard_map/all_gather | solution.py:41
  7.3 120.7 %all-gather.5.cloned.1.call-start = ((), (), s32[]{:S(2)}) async-start(), calls=%async_computation.2 | async-start | bytes 2359296 | tf_op jit(solution)/shard_map/all_gather | solution.py:42
  8.0 122.9 %all-gather.7.cloned.1.call-start = ((), (), s32[]{:S(2)}) async-start(), calls=%async_computation.3 | async-start | bytes 2359296 | tf_op jit(solution)/shard_map/all_gather | solution.py:40
  9.6 2.0 %copy-start.5 = (s32[32]{0:T(128)S(1)}, s32[32]{0:T(128)}, u32[]{:S(2)}) copy-start(s32[32]{0:T(128)} %param.24) | copy-start | bytes 388
  9.6 2.3 %copy-start.4 = (s32[32,8]{0,1:T(8,128)S(1)}, s32[32,8]{0,1:T(8,128)}, u32[]{:S(2)}) copy-start(s32[32,8]{0,1:T(8,128)} %param.23) | copy-start | bytes 3076
  56.9 38.1 %all-to-all-start = ((bf16[8,128,1024]{2,1,0:T(8,128)(2,1)}), bf16[8,128,1024]{2,1,0:T(8,128)(2,1)}, u32[]{:S(2)}, u32[]{:S(2)}) async-start(bf16[8,128,1024]{2,1,0:T(8,128)(2,1)} %get-tuple-element.22), calls=%async_computation | async-start | bytes 4194304 | tf_op jit(solution)/shard_map/all_to_all | solution.py:69
  61.3 93.9 %all-gather.11.cloned.1.call-start = ((), (), s32[]{:S(2)}) async-start(), calls=%async_computation.5 | async-start | bytes 2359296 | tf_op jit(solution)/shard_map/all_gather | solution.py:133
  97.9 16.9 %collective-permute-start = (bf16[2,128,1024]{2,1,0:T(8,128)(2,1)}, bf16[2,128,1024]{2,1,0:T(8,128)(2,1)}, u32[]{:S(2)}, u32[]{:S(2)}) collective-permute-start(bf16[2,128,1024]{2,1,0:T(8,128)(2,1)} %pad_maximum_fusion), channel_id=1, source_target_pairs={{24,0},{0,8},{8,16},{16,24},{25,1},{1,9},{9,17},{17,25},{26,2},{2,... | collective-permute-start | bytes 1572872 | tf_op jit(solution)/shard_map/ppermute | solution.py:13
  100.3 21.8 %collective-permute-start.1 = (bf16[2,128,1024]{2,1,0:T(8,128)(2,1)}, bf16[2,128,1024]{2,1,0:T(8,128)(2,1)}, u32[]{:S(2)}, u32[]{:S(2)}) collective-permute-start(bf16[2,128,1024]{2,1,0:T(8,128)(2,1)} %pad_maximum_fusion.1), channel_id=1, source_target_pairs={{8,0},{16,8},{24,16},{0,24},{9,1},{17,9},{25,17},{1,25},{10,2},{18... | collective-permute-start | bytes 1572872 | tf_op jit(solution)/shard_map/ppermute | solution.py:13
  115.8 9.3 %copy-start.2 = (bf16[128,1024]{1,0:T(8,128)(2,1)S(1)}, bf16[128,1024]{1,0:T(8,128)(2,1)}, u32[]{:S(2)}) copy-start(bf16[128,1024]{1,0:T(8,128)(2,1)} %param.15) | copy-start | bytes 786436
  133.0 5.0 %copy-start.3 = (bf16[1,768,8,128]{1,3,2,0:T(8,128)(2,1)S(1)}, bf16[1,768,8,128]{1,3,2,0:T(8,128)(2,1)}, u32[]{:S(2)}) copy-start(bf16[1,768,8,128]{1,3,2,0:T(8,128)(2,1)} %copy.56) | copy-start | bytes 4718596
Sparse Core Ops, SparseCore 0:
  9.2 41.8 all-gather.8
  53.0 40.6 all-gather.4
  95.6 29.6 all-gather.6
  127.0 28.0 all-gather.10
where the time goes:
time: 165 us; the launch traced here: 164 us
  waiting for transfers between devices  50 us (30%)
  blocking collectives  37.2 us (23%)
  local copies, waits for them, and re-layouts  26.1 us (16%)
  between operations  17 us (10%)
  matrix products  16.6 us (10%)
  other arithmetic  9.24 us (6%)
  starting transfers between devices  8.33 us (5%)
    all_to_all x1, blocking collectives, per_device(): lax.all_to_all(offer_values, 'tok', split_axis=0, concat_axis=0, tiled=True)  37.2 us
    all_to_all x1, waiting for transfers between devices, per_device(): lax.all_to_all(offer_keys, 'tok', split_axis=0, concat_axis=0, tiled=True)  26.7 us
    all_gather x1, waiting for transfers between devices, per_device(): whole_out = lax.all_gather(w_out, 'tok', axis=1, tiled=True)  14.5 us
    ppermute x2, waiting for transfers between devices, shifted(): return lax.ppermute(block, axis, route)  6.26 us
    sub x1, matrix products, per_device(): scores - row_max  4.96 us
    all_to_all x1, starting transfers between devices, per_device(): lax.all_to_all(offer_keys, 'tok', split_axis=0, concat_axis=0, tiled=True)  4.38 us
    ppermute x2, starting transfers between devices, shifted(): return lax.ppermute(block, axis, route)  3.82 us
    gather x1, local copies, waits for them, and re-layouts, per_device(): jnp.take(got_keys, own_index, axis=0)  3.47 us
  transfers between devices with their start and end apart: 7, of which 4 were waited for; matrix products, arithmetic and copies ran while one was open for 30% of the time, Pallas kernels for 0%

commit v1 on v0

--- a/solution.py
+++ b/solution.py
@@ -5,6 +5,35 @@
 
 HEADS = 8
 QB = 128
+
+
+def _pair_trees(view, dim_k, array_in):
+    a_now, r1 = (view.shape[:dim_k], view.shape[dim_k + 1 :])
+    return jnp.moveaxis(view.reshape(*a_now, array_in, -1, *r1), dim_k, 0)
+
+
+def fill_page(inp, array_dim):
+    local_now = list(inp.shape[1:])
+    local_now[array_dim] *= inp.shape[0]
+    return jnp.moveaxis(inp, 0, array_dim).reshape(local_now)
+
+
+def bind_shards(dev_axis, here_x, xs, payload):
+    arr_next = lax.psum(1, axis_name=dev_axis)
+    spare, new = (arr_next, lax.axis_index(dev_axis))
+    current_arr = _pair_trees(xs, payload, spare)
+    panels = [current_arr[new]]
+    idx = 1
+    while idx < spare:
+        piece_now = current_arr[(new + idx) % spare]
+        left_arr = lax.ppermute(
+            piece_now, axis_name=dev_axis, perm=[(kk, (kk + idx) % spare) for kk in range(spare)]
+        )
+        panels.append(left_arr)
+        idx = idx + 1
+    block_out = jnp.stack(panels)
+    current_arr = block_out[(new - jnp.arange(spare)) % spare]
+    return fill_page(current_arr, here_x)
 
 
 def shifted(block, axis, distance):
@@ -67,7 +96,7 @@
     my_tok_table = lax.dynamic_slice_in_dim(source_tok, my_start, blocks_dev, 0)
     got_keys, got_values = (
         lax.all_to_all(offer_keys, "tok", split_axis=0, concat_axis=0, tiled=True),
-        lax.all_to_all(offer_values, "tok", split_axis=0, concat_axis=0, tiled=True),
+        bind_shards("tok", 0, offer_values, 0),
     )
     upward_index = lax.dynamic_index_in_dim(
         lead_tok[:, 0], upper_region * n_tok + tok_id, 0, keepdims=False

time: 165 us -> 160 us (0.970)
  blocking collectives: 37.2 us -> 0 us
  local copies, waits for them, and re-layouts: 26.1 us -> 43.5 us
  starting transfers between devices: 8.33 us -> 17.4 us
  waiting for transfers between devices: 50 us -> 54 us
    all_to_all x1 -> x0, blocking collectives: 37.2 us -> none  [per_device(): lax.all_to_all(offer_values, 'tok', split_axis=0, concat_axis=0, tiled=True)]
    ppermute x0 -> x7, waiting for transfers between devices: none -> 29.1 us  [bind_shards(): lax.ppermute(piece_now, axis_name=dev_axis, perm=[(kk, (kk + idx) % spare...]
    all_to_all x1, waiting for transfers between devices: 26.7 us -> 0.01 us  [per_device(): lax.all_to_all(offer_keys, 'tok', split_axis=0, concat_axis=0, tiled=True)]
    unnamed x19 -> x28, local copies, waits for them, and re-layouts: 1.87 us -> 13 us
    ppermute x0 -> x7, starting transfers between devices: none -> 9.53 us  [bind_shards(): lax.ppermute(piece_now, axis_name=dev_axis, perm=[(kk, (kk + idx) % spare...]
    gather x0 -> x1, local copies, waits for them, and re-layouts: none -> 3.65 us  [bind_shards(): current_arr = block_out[(new - jnp.arange(spare)) % spare]]
    ppermute x2, waiting for transfers between devices: 6.26 us -> 9.26 us  [shifted(): return lax.ppermute(block, axis, route)]
  transfers between devices with their start and end apart: 7 -> 14, of which waited for: 4 -> 6; matrix products, arithmetic and copies ran while one was open for 30% -> 42% of each run, Pallas kernels for 0% -> 0%
where the time goes in v1:
time: 160 us; the launch traced here: 159 us
  waiting for transfers between devices  54 us (34%)
  local copies, waits for them, and re-layouts  43.5 us (27%)
  starting transfers between devices  17.4 us (11%)
  between operations  17.2 us (11%)
  matrix products  16.6 us (10%)
  other arithmetic  10.2 us (6%)
    ppermute x7, waiting for transfers between devices, bind_shards(): lax.ppermute(piece_now, axis_name=dev_axis, perm=[(kk, (kk + idx) % spare...  29.1 us
    all_gather x1, waiting for transfers between devices, per_device(): whole_out = lax.all_gather(w_out, 'tok', axis=1, tiled=True)  13 us
    unnamed x28, local copies, waits for them, and re-layouts  13 us
    ppermute x7, starting transfers between devices, bind_shards(): lax.ppermute(piece_now, axis_name=dev_axis, perm=[(kk, (kk + idx) % spare...  9.53 us
    ppermute x2, waiting for transfers between devices, shifted(): return lax.ppermute(block, axis, route)  9.26 us
    sub x1, matrix products, per_device(): scores - row_max  4.94 us
    all_to_all x1, starting transfers between devices, per_device(): lax.all_to_all(offer_keys, 'tok', split_axis=0, concat_axis=0, tiled=True)  3.92 us
    ppermute x2, starting transfers between devices, shifted(): return lax.ppermute(block, axis, route)  3.82 us
  transfers between devices with their start and end apart: 14, of which 6 were waited for; matrix products, arithmetic and copies ran while one was open for 42% of the time, Pallas kernels for 0%

profile of v1, /device:TPU:0, one launch (start us, length us, event | category | flops | bytes accessed | tf_op | source)
XLA Modules:
  0.0 158.8 jit_solution(5213950817103844096)
XLA Ops:
  9.7 1.9 %gather_fusion = s32[256]{0:T(256)S(1)} fusion(s32[32]{0:T(128)S(1)} %copy-done.1, s32[1024]{0:T(1024)S(1)} %pad_clamp_fusion.3), kind=kCustom, calls=%fused_computation.4 | custom fusion | bytes 3072 | tf_op jit(solution)/shard_map/jit(_take)/gather | solution.py:79
  13.1 3.2 %gather_fusion.3 = bf16[8,128,1024]{2,1,0:T(8,128)(2,1)} fusion(bf16[4,128,1024]{2,1,0:T(8,128)(2,1)} %param.21, s32[1024]{0:T(1024)S(1)} %pad_clamp_fusion.2), kind=kCustom, calls=%fused_computation.2.clone | custom fusion | bytes 4194336 | tf_op jit(solution)/shard_map/jit(_take)/gather | solution.py:91
  16.3 3.3 %broadcast_select_fusion = (bf16[8,128,1024]{2,1,0:T(8,128)(2,1)S(1)}, bf16[8,128,1024]{2,1,0:T(8,128)(2,1)}) fusion(bf16[8,128,1024]{2,1,0:T(8,128)(2,1)} %gather_fusion.3, pred[8]{0:T(512)(128)(4,1)S(1)} %compare_and_fusion.1, bf16[8,128,1024]{2,1,0:T(8,128)(2,1)S(1)} %gather_fusion.2), kind=kLoop, calls=%fused_computation.27 | loop fusion | flops 2097152 | bytes 8388616 | tf_op jit(solution)/shard_map/jit(_take)/select_n | solution.py:91
  22.7 2.6 %collective-permute-start.1 = (bf16[1,128,1024]{2,1,0:T(8,128)(2,1)}, bf16[1,128,1024]{2,1,0:T(8,128)(2,1)}, u32[]{:S(2)}, u32[]{:S(2)}) collective-permute-start(bf16[1,128,1024]{2,1,0:T(8,128)(2,1)} %get-tuple-element.18), channel_id=1, source_target_pairs={{0,2},{1,3},{2,4},{3,5},{4,6},{5,7},{6,0},{7,1},{8,10},{9,11},{10,... | collective-permute-start | bytes 786440 | tf_op jit(solution)/shard_map/ppermute | solution.py:29
  25.3 2.4 %collective-permute-start.2 = (bf16[1,128,1024]{2,1,0:T(8,128)(2,1)}, bf16[1,128,1024]{2,1,0:T(8,128)(2,1)}, u32[]{:S(2)}, u32[]{:S(2)}) collective-permute-start(bf16[1,128,1024]{2,1,0:T(8,128)(2,1)} %get-tuple-element.17), channel_id=1, source_target_pairs={{0,3},{1,4},{2,5},{3,6},{4,7},{5,0},{6,1},{7,2},{8,11},{9,12},{10,... | collective-permute-start | bytes 786440 | tf_op jit(solution)/shard_map/ppermute | solution.py:29
  28.3 3.9 %all-to-all-start = ((bf16[8,128,1024]{2,1,0:T(8,128)(2,1)}), bf16[8,128,1024]{2,1,0:T(8,128)(2,1)S(1)}, u32[]{:S(2)}, u32[]{:S(2)}) async-start(bf16[8,128,1024]{2,1,0:T(8,128)(2,1)} %get-tuple-element.29), calls=%async_computation | async-start | bytes 4194304 | tf_op jit(solution)/shard_map/all_to_all | solution.py:98
  40.4 3.0 %collective-permute-start.5 = (bf16[1,128,1024]{2,1,0:T(8,128)(2,1)}, bf16[1,128,1024]{2,1,0:T(8,128)(2,1)S(1)}, u32[]{:S(2)}, u32[]{:S(2)}) collective-permute-start(bf16[1,128,1024]{2,1,0:T(8,128)(2,1)} %get-tuple-element.14), channel_id=1, source_target_pairs={{0,6},{1,7},{2,0},{3,1},{4,2},{5,3},{6,4},{7,5},{8,14},{9,15},{10,... | collective-permute-start | bytes 786440 | tf_op jit(solution)/shard_map/ppermute | solution.py:29
  47.2 2.2 %collective-permute-done.2 = bf16[1,128,1024]{2,1,0:T(8,128)(2,1)} collective-permute-done((bf16[1,128,1024]{2,1,0:T(8,128)(2,1)}, bf16[1,128,1024]{2,1,0:T(8,128)(2,1)}, u32[]{:S(2)}, u32[]{:S(2)}) %collective-permute-start.2) | collective-permute-done | bytes 262176 | tf_op jit(solution)/shard_map/ppermute | solution.py:29
  52.7 8.1 %collective-permute-done.4 = bf16[1,128,1024]{2,1,0:T(8,128)(2,1)S(1)} collective-permute-done((bf16[1,128,1024]{2,1,0:T(8,128)(2,1)}, bf16[1,128,1024]{2,1,0:T(8,128)(2,1)S(1)}, u32[]{:S(2)}, u32[]{:S(2)}) %collective-permute-start.4) | collective-permute-done | bytes 262176 | tf_op jit(solution)/shard_map/ppermute | solution.py:29
  61.5 14.9 %collective-permute-done.5 = bf16[1,128,1024]{2,1,0:T(8,128)(2,1)S(1)} collective-permute-done((bf16[1,128,1024]{2,1,0:T(8,128)(2,1)}, bf16[1,128,1024]{2,1,0:T(8,128)(2,1)S(1)}, u32[]{:S(2)}, u32[]{:S(2)}) %collective-permute-start.5) | collective-permute-done | bytes 262176 | tf_op jit(solution)/shard_map/ppermute | solution.py:29
  77.1 4.0 %collective-permute-done.6 = bf16[1,128,1024]{2,1,0:T(8,128)(2,1)S(1)} collective-permute-done((bf16[1,128,1024]{2,1,0:T(8,128)(2,1)}, bf16[1,128,1024]{2,1,0:T(8,128)(2,1)S(1)}, u32[]{:S(2)}, u32[]{:S(2)}) %collective-permute-start.6) | collective-permute-done | bytes 262176 | tf_op jit(solution)/shard_map/ppermute | solution.py:29
  81.8 3.7 %gather_fusion.1 = bf16[8,128,1024]{2,1,0:T(8,128)(2,1)} fusion(bf16[8,128,1024]{2,1,0:T(8,128)(2,1)} %bitcast.111, s32[1024]{0:T(1024)S(1)} %pad_clamp_fusion.1), kind=kCustom, calls=%fused_computation.5 | custom fusion | bytes 4194336 | tf_op jit(solution)/shard_map/gather | solution.py:35
  91.2 3.4 %gather_fusion.4 = bf16[6,128,1024]{2,1,0:T(8,128)(2,1)} fusion(bf16[8,128,1024]{2,1,0:T(8,128)(2,1)} %gather_fusion.1, s32[1024]{0:T(1024)S(1)} %pad_clamp_fusion), kind=kCustom, calls=%fused_computation.1.clone | custom fusion | bytes 3145752 | tf_op jit(solution)/shard_map/jit(_take)/gather | solution.py:127
  96.4 2.4 %collective-permute-start.8 = (bf16[2,128,1024]{2,1,0:T(8,128)(2,1)}, bf16[2,128,1024]{2,1,0:T(8,128)(2,1)}, u32[]{:S(2)}, u32[]{:S(2)}) collective-permute-start(bf16[2,128,1024]{2,1,0:T(8,128)(2,1)} %pad_maximum_fusion.1), channel_id=1, source_target_pairs={{8,0},{16,8},{24,16},{0,24},{9,1},{17,9},{25,17},{1,25},{10,2},{18... | collective-permute-start | bytes 1572872 | tf_op jit(solution)/shard_map/ppermute | solution.py:42
  98.9 1.9 %gather_fusion.5 = bf16[6,128,1024]{2,1,0:T(8,128)(2,1)} fusion(bf16[8,128,1024]{2,1,0:T(8,128)(2,1)S(1)} %all-to-all-done, s32[1024]{0:T(1024)S(1)} %pad_clamp_fusion), kind=kCustom, calls=%fused_computation.3.clone | custom fusion | bytes 3145752 | tf_op jit(solution)/shard_map/jit(_take)/gather | solution.py:124
  100.8 2.2 %broadcast_select_fusion.3 = (bf16[6,128,1024]{2,1,0:T(8,128)(2,1)S(1)}, bf16[6,128,1024]{2,1,0:T(8,128)(2,1)S(1)}) fusion(bf16[6,128,1024]{2,1,0:T(8,128)(2,1)} %gather_fusion.4, pred[6]{0:T(512)(128)(4,1)S(1)} %get-tuple-element.6, bf16[6,128,1024]{2,1,0:T(8,128)(2,1)} %gather_fusion.5), kind=kLoop, calls=%fused_computation.30 | loop fusion | flops 1572864 | bytes 6291462 | tf_op jit(solution)/shard_map/jit(_take)/select_n | solution.py:127
  108.6 9.3 %collective-permute-done.8 = bf16[2,128,1024]{2,1,0:T(8,128)(2,1)} collective-permute-done((bf16[2,128,1024]{2,1,0:T(8,128)(2,1)}, bf16[2,128,1024]{2,1,0:T(8,128)(2,1)}, u32[]{:S(2)}, u32[]{:S(2)}) %collective-permute-start.8) | collective-permute-done | bytes 524320 | tf_op jit(solution)/shard_map/ppermute | solution.py:42
  121.0 2.0 %fusion.21 = bf16[16,8,8,128]{3,1,2,0:T(8,128)(2,1)S(1)} fusion(bf16[128,1024]{1,0:T(8,128)(2,1)S(1)} %copy-done.3, bf16[1024,1024]{1,0:T(8,128)(2,1)} %all-gather.9.cloned.1.call-done), kind=kOutput, calls=%fused_computation.37 | convolution fusion | flops 268566528 | bytes 2621440 | tf_op jit(solution)/shard_map/dot_general | solution.py:74
  123.8 2.0 %convolution_convert_fusion.3 = bf16[128,1024]{1,0:T(8,128)(2,1)S(1)} fusion(bf16[128,1024]{1,0:T(8,128)(2,1)S(1)} %copy-done.3, bf16[1024,1024]{1,0:T(8,128)(2,1)} %all-gather.5.cloned.1.call-done), kind=kOutput, calls=%fused_computation.35 | convolution fusion | flops 268566528 | bytes 2621440 | tf_op jit(solution)/shard_map/dot_general | solution.py:75
  126.7 2.1 %fusion.20 = bf16[16,8,8,128]{3,2,1,0:T(8,128)(2,1)S(1)} fusion(bf16[128,1024]{1,0:T(8,128)(2,1)S(1)} %copy-done.3, bf16[1024,1024]{1,0:T(8,128)(2,1)} %all-gather.7.cloned.1.call-done), kind=kOutput, calls=%fused_computation.36 | convolution fusion | flops 268566528 | bytes 2621440 | tf_op jit(solution)/shard_map/dot_general | solution.py:73
  128.8 4.9 %fusion.40 = (f32[8,128]{1,0:T(8,128)S(1)}, bf16[8,128,1152]{2,1,0:T(8,128)(2,1)}) fusion(pred[1152]{0:T(1024)(128)(4,1)S(1)} %pad_reduce_fusion, bf16[1,768,8,128]{3,1,2,0:T(8,128)(2,1)} %copy.74, bf16[1,128,8,128]{3,1,2,0:T(8,128)(2,1)} %copy.73, bf16[1,128,8,128]{3,1,2,0:T(8,128)(2,1)S(1)} %copy.72, bf16[1,128,8,128]{3,1,2,0:T(8,128)(2,1)} %copy.71, ...), kind=kOutput, calls=%fused_computation.101 | convolution fusion | flops 318506112 | bytes 4985984 | tf_op jit(solution)/shard_map/sub | solution.py:153
  133.8 2.7 %fusion.25 = bf16[1,128,8,128]{1,3,2,0:T(8,128)(2,1)S(1)} fusion(bf16[8,128,1152]{2,1,0:T(8,128)(2,1)} %get-tuple-element.31, bf16[1,768,8,128]{1,3,2,0:T(8,128)(2,1)S(1)} %copy-done.4, bf16[1,128,8,128]{1,3,2,0:T(8,128)(2,1)} %bitcast.117, bf16[1,128,8,128]{1,3,2,0:T(8,128)(2,1)S(1)} %bitcast.116, bf16[1,128,8,128]{1,3,2,0:T(8,128)(2,1)} %bitcast.118, ...), kind=kOutput, calls=%fused_computation.39 | convolution fusion | flops 311689216 | bytes 4984832 | tf_op jit(solution)/shard_map/bhqk,bkhd->bqhd/dot_general | solution.py:157
  136.5 13.0 %all-gather.11.cloned.1.call-done = bf16[1024,1024]{1,0:T(8,128)(2,1)} async-done(((bf16[1024,128]{1,0:T(8,128)(2,1)}), bf16[1024,1024]{1,0:T(8,128)(2,1)}) %all-gather.11.cloned.1.call-update) | async-done | bytes 2097168 | tf_op jit(solution)/shard_map/all_gather | solution.py:162
  149.5 2.8 %convolution_convert_fusion = bf16[128,1024]{1,0:T(8,128)(2,1)} fusion(bf16[128,1024]{0,1:T(8,128)(2,1)S(1)} %bitcast.115, bf16[1024,1024]{1,0:T(8,128)(2,1)} %all-gather.11.cloned.1.call-done), kind=kOutput, calls=%fused_computation.32 | convolution fusion | flops 268566528 | bytes 2621440 | tf_op jit(solution)/shard_map/dot_general | solution.py:163
  (94 shorter events, 39.8 us)
Async XLA Ops:
  6.5 5.8 %copy-start = (bf16[4,128,1024]{2,1,0:T(8,128)(2,1)S(1)}, bf16[4,128,1024]{2,1,0:T(8,128)(2,1)}, u32[]{:S(2)}) copy-start(bf16[4,128,1024]{2,1,0:T(8,128)(2,1)} %param.20) | copy-start | bytes 3145732
  6.5 3.2 %copy-start.1 = (s32[32]{0:T(128)S(1)}, s32[32]{0:T(128)}, u32[]{:S(2)}) copy-start(s32[32]{0:T(128)} %param.25) | copy-start | bytes 388
  6.5 114.4 %all-gather.9.cloned.1.call-start = ((), (), s32[]{:S(2)}) async-start(), calls=%async_computation.3 | async-start | bytes 2359296 | tf_op jit(solution)/shard_map/all_gather | solution.py:70
  7.3 116.6 %all-gather.5.cloned.1.call-start = ((), (), s32[]{:S(2)}) async-start(), calls=%async_computation.1 | async-start | bytes 2359296 | tf_op jit(solution)/shard_map/all_gather | solution.py:71
  8.0 118.7 %all-gather.7.cloned.1.call-start = ((), (), s32[]{:S(2)}) async-start(), calls=%async_computation.2 | async-start | bytes 2359296 | tf_op jit(solution)/shard_map/all_gather | solution.py:69
  9.7 2.0 %copy-start.6 = (s32[32]{0:T(128)S(1)}, s32[32]{0:T(128)}, u32[]{:S(2)}) copy-start(s32[32]{0:T(128)} %param.24) | copy-start | bytes 388
  9.7 2.3 %copy-start.5 = (s32[32,8]{0,1:T(8,128)S(1)}, s32[32,8]{0,1:T(8,128)}, u32[]{:S(2)}) copy-start(s32[32,8]{0,1:T(8,128)} %param.23) | copy-start | bytes 3076
  19.6 1.4 copy-start.2
  22.2 18.1 %collective-permute-start = (bf16[1,128,1024]{2,1,0:T(8,128)(2,1)}, bf16[1,128,1024]{2,1,0:T(8,128)(2,1)}, u32[]{:S(2)}, u32[]{:S(2)}) collective-permute-start(bf16[1,128,1024]{2,1,0:T(8,128)(2,1)} %get-tuple-element.19), channel_id=1, source_target_pairs={{0,1},{1,2},{2,3},{3,4},{4,5},{5,6},{6,7},{7,0},{8,9},{9,10},{10,1... | collective-permute-start | bytes 786440 | tf_op jit(solution)/shard_map/ppermute | solution.py:29
  22.7 22.3 %collective-permute-start.1 = (bf16[1,128,1024]{2,1,0:T(8,128)(2,1)}, bf16[1,128,1024]{2,1,0:T(8,128)(2,1)}, u32[]{:S(2)}, u32[]{:S(2)}) collective-permute-start(bf16[1,128,1024]{2,1,0:T(8,128)(2,1)} %get-tuple-element.18), channel_id=1, source_target_pairs={{0,2},{1,3},{2,4},{3,5},{4,6},{5,7},{6,0},{7,1},{8,10},{9,11},{10,... | collective-permute-start | bytes 786440 | tf_op jit(solution)/shard_map/ppermute | solution.py:29
  25.3 24.1 %collective-permute-start.2 = (bf16[1,128,1024]{2,1,0:T(8,128)(2,1)}, bf16[1,128,1024]{2,1,0:T(8,128)(2,1)}, u32[]{:S(2)}, u32[]{:S(2)}) collective-permute-start(bf16[1,128,1024]{2,1,0:T(8,128)(2,1)} %get-tuple-element.17), channel_id=1, source_target_pairs={{0,3},{1,4},{2,5},{3,6},{4,7},{5,0},{6,1},{7,2},{8,11},{9,12},{10,... | collective-permute-start | bytes 786440 | tf_op jit(solution)/shard_map/ppermute | solution.py:29
  27.7 23.3 %collective-permute-start.3 = (bf16[1,128,1024]{2,1,0:T(8,128)(2,1)}, bf16[1,128,1024]{2,1,0:T(8,128)(2,1)}, u32[]{:S(2)}, u32[]{:S(2)}) collective-permute-start(bf16[1,128,1024]{2,1,0:T(8,128)(2,1)} %get-tuple-element.16), channel_id=1, source_target_pairs={{0,4},{1,5},{2,6},{3,7},{4,0},{5,1},{6,2},{7,3},{8,12},{9,13},{10,... | collective-permute-start | bytes 786440 | tf_op jit(solution)/shard_map/ppermute | solution.py:29
  28.2 32.6 %collective-permute-start.4 = (bf16[1,128,1024]{2,1,0:T(8,128)(2,1)}, bf16[1,128,1024]{2,1,0:T(8,128)(2,1)S(1)}, u32[]{:S(2)}, u32[]{:S(2)}) collective-permute-start(bf16[1,128,1024]{2,1,0:T(8,128)(2,1)} %get-tuple-element.15), channel_id=1, source_target_pairs={{0,5},{1,6},{2,7},{3,0},{4,1},{5,2},{6,3},{7,4},{8,13},{9,14},{10,... | collective-permute-start | bytes 786440 | tf_op jit(solution)/shard_map/ppermute | solution.py:29
  28.3 59.0 %all-to-all-start = ((bf16[8,128,1024]{2,1,0:T(8,128)(2,1)}), bf16[8,128,1024]{2,1,0:T(8,128)(2,1)S(1)}, u32[]{:S(2)}, u32[]{:S(2)}) async-start(bf16[8,128,1024]{2,1,0:T(8,128)(2,1)} %get-tuple-element.29), calls=%async_computation | async-start | bytes 4194304 | tf_op jit(solution)/shard_map/all_to_all | solution.py:98
  32.2 117.4 %all-gather.11.cloned.1.call-start = ((), (), s32[]{:S(2)}) async-start(), calls=%async_computation.4 | async-start | bytes 2359296 | tf_op jit(solution)/shard_map/all_gather | solution.py:162
  40.4 36.0 %collective-permute-start.5 = (bf16[1,128,1024]{2,1,0:T(8,128)(2,1)}, bf16[1,128,1024]{2,1,0:T(8,128)(2,1)S(1)}, u32[]{:S(2)}, u32[]{:S(2)}) collective-permute-start(bf16[1,128,1024]{2,1,0:T(8,128)(2,1)} %get-tuple-element.14), channel_id=1, source_target_pairs={{0,6},{1,7},{2,0},{3,1},{4,2},{5,3},{6,4},{7,5},{8,14},{9,15},{10,... | collective-permute-start | bytes 786440 | tf_op jit(solution)/shard_map/ppermute | solution.py:29
  45.0 36.1 %collective-permute-start.6 = (bf16[1,128,1024]{2,1,0:T(8,128)(2,1)}, bf16[1,128,1024]{2,1,0:T(8,128)(2,1)S(1)}, u32[]{:S(2)}, u32[]{:S(2)}) collective-permute-start(bf16[1,128,1024]{2,1,0:T(8,128)(2,1)} %get-tuple-element.13), channel_id=1, source_target_pairs={{0,7},{1,0},{2,1},{3,2},{4,3},{5,4},{6,5},{7,6},{8,15},{9,8},{10,9... | collective-permute-start | bytes 786440 | tf_op jit(solution)/shard_map/ppermute | solution.py:29
  89.8 17.4 %collective-permute-start.7 = (bf16[2,128,1024]{2,1,0:T(8,128)(2,1)}, bf16[2,128,1024]{2,1,0:T(8,128)(2,1)}, u32[]{:S(2)}, u32[]{:S(2)}) collective-permute-start(bf16[2,128,1024]{2,1,0:T(8,128)(2,1)} %pad_maximum_fusion), channel_id=1, source_target_pairs={{24,0},{0,8},{8,16},{16,24},{25,1},{1,9},{9,17},{17,25},{26,2},{2,... | collective-permute-start | bytes 1572872 | tf_op jit(solution)/shard_map/ppermute | solution.py:42
  96.4 21.4 %collective-permute-start.8 = (bf16[2,128,1024]{2,1,0:T(8,128)(2,1)}, bf16[2,128,1024]{2,1,0:T(8,128)(2,1)}, u32[]{:S(2)}, u32[]{:S(2)}) collective-permute-start(bf16[2,128,1024]{2,1,0:T(8,128)(2,1)} %pad_maximum_fusion.1), channel_id=1, source_target_pairs={{8,0},{16,8},{24,16},{0,24},{9,1},{17,9},{25,17},{1,25},{10,2},{18... | collective-permute-start | bytes 1572872 | tf_op jit(solution)/shard_map/ppermute | solution.py:42
  108.2 12.8 %copy-start.3 = (bf16[128,1024]{1,0:T(8,128)(2,1)S(1)}, bf16[128,1024]{1,0:T(8,128)(2,1)}, u32[]{:S(2)}) copy-start(bf16[128,1024]{1,0:T(8,128)(2,1)} %param.15) | copy-start | bytes 786436
  128.8 5.0 %copy-start.4 = (bf16[1,768,8,128]{1,3,2,0:T(8,128)(2,1)S(1)}, bf16[1,768,8,128]{1,3,2,0:T(8,128)(2,1)}, u32[]{:S(2)}) copy-start(bf16[1,768,8,128]{1,3,2,0:T(8,128)(2,1)} %copy.68) | copy-start | bytes 4718596
Sparse Core Ops, SparseCore 0:
  9.2 41.9 all-gather.8
  53.1 35.3 all-gather.4
  90.4 29.2 all-gather.6
  121.4 28.0 all-gather.10
